TPU v7x, 32 devices: a whole 2x2x4 slice. The times are simulated.
32 devices in a mesh: tp: 4 (over y, x), row: 4 (over z), col: 2 (over core).
Axes of the slice: x: 2, y: 2, z: 4, core: 2. Of those that a mesh axis runs over, the one named last changes fastest.
Arguments:
- hidden: bfloat16 [128, 14336], P('col', 'row'), may hold values from -6 to 6
- out_grad: bfloat16 [128, 4096], P(None, ('tp', 'row')), may hold values from -6 to 6
- basis_in: bfloat16 [14336, 4096], P(('row', 'col'), 'tp'), may hold values from -0.046875 to 0.046875
- basis_out: bfloat16 [4096, 1024], P(('tp', 'row'), 'col'), may hold values from -0.09375 to 0.09375
- eigen: float32 [4096, 1024], P(('tp', 'row'), 'col'), may hold values from 0.02 to 2
Outputs:
- precond: float32 [4096, 14336], P(('tp', 'col'), 'row')
All inputs are finite; a program needn't handle non-finite values.
Results may differ from a plain program's by a relative error of at most 0.024.
Values may be sent and summed in bfloat16 or wider, within the bound.
No kernel may reach another device: no remote copies, remote signals or barrier semaphores. Data moves between devices by JAX's collectives and lax.ppermute only.
A program may use at most 64 MiB of HBM per device.

v0:
```python
import jax
import jax.numpy as jnp
from jax import lax
from jax.sharding import PartitionSpec as P

damping = 0.01


def contract_rows(left, right):
    return lax.dot_general(
        left, right, (((0,), (0,)), ((), ())), preferred_element_type=jnp.float32
    )


def contract_cols(left, right):
    return lax.dot_general(
        left, right, (((1,), (1,)), ((), ())), preferred_element_type=jnp.float32
    )


def shards(hidden, out_grad, basis_in, basis_out, eigen):
    tp_count = lax.axis_size("tp")
    col_count = lax.axis_size("col")
    basis_block = lax.all_gather(basis_in, "col", axis=0, tiled=True)
    partial_in = jnp.dot(hidden, basis_block, preferred_element_type=jnp.float32)
    rotated_in = lax.psum_scatter(
        partial_in.astype(jnp.bfloat16), "row", scatter_dimension=1, tiled=True
    )
    rotated_in = lax.all_gather(rotated_in, "col", axis=0, tiled=True)
    queries = rotated_in.shape[0]
    partial_out = jnp.dot(out_grad, basis_out, preferred_element_type=jnp.float32)
    rotated_out = lax.psum(partial_out, ("tp", "row")).astype(jnp.bfloat16)
    coeff = contract_rows(rotated_in, rotated_out)
    scaled = (coeff / (queries * (eigen + damping))).astype(jnp.bfloat16)
    mixed_part = contract_cols(scaled, lax.all_gather(basis_out, ("tp", "row"), axis=0, tiled=True))
    depth = mixed_part.shape[0]
    width = mixed_part.shape[1]
    mixed_part = mixed_part.reshape(depth, tp_count, col_count, width // (tp_count * col_count))
    mixed = lax.psum_scatter(
        mixed_part.astype(jnp.bfloat16), "col", scatter_dimension=2, tiled=True
    ).astype(jnp.float32)
    mixed = mixed.reshape(depth, width // col_count).astype(jnp.bfloat16)
    mixed = lax.all_gather(mixed, "row", axis=0, tiled=True)
    return lax.psum_scatter(
        lax.dot_general(
            mixed, basis_block, (((0,), (1,)), ((), ())), preferred_element_type=jnp.float32
        ).astype(jnp.bfloat16),
        "tp",
        scatter_dimension=0,
        tiled=True,
    ).astype(jnp.float32)


def solution(mesh):
    placed = (
        P("col", "row"),
        P(None, ("tp", "row")),
        P(("row", "col"), "tp"),
        P(("tp", "row"), "col"),
        P(("tp", "row"), "col"),
    )
    return jax.shard_map(
        shards, mesh=mesh, in_specs=placed, out_specs=P(("tp", "col"), "row"), check_vma=False
    )
```

profile of v0, /device:TPU:0, one launch (start us, length us, event | category | flops | bytes accessed | tf_op | source)
XLA Modules:
  0.0 397.8 jit_solution(9604397828768367093)
XLA Ops:
  7.4 0.0 copy-start
  7.4 0.0 all-gather.4.cloned.1.call-start
  7.4 0.7 all-gather.4.cloned.1.call-update
  8.1 0.0 copy-start.1
  8.1 0.0 copy-start.2
  8.1 0.0 copy-start.3
  8.1 0.0 reduce-scatter.4.cloned.1.call-start
  8.2 22.6 %all-gather.4.cloned.1.call-done = bf16[3584,1024]{1,0:T(8,128)(2,1)} async-done(((bf16[1792,1024]{1,0:T(8,128)(2,1)}), bf16[3584,1024]{1,0:T(8,128)(2,1)}) %all-gather.4.cloned.1.call-update) | async-done | bytes 7340048 | tf_op jit(solution)/shard_map/all_gather | solution.py:24
  30.8 0.0 copy-done
  30.8 5.1 %convolution_convert_fusion.2 = bf16[64,1024]{1,0:T(8,128)(2,1)} fusion(bf16[64,3584]{1,0:T(8,128)(2,1)S(1)} %copy-done, bf16[3584,1024]{1,0:T(8,128)(2,1)} %all-gather.4.cloned.1.call-done), kind=kOutput, calls=%fused_computation.4 | convolution fusion | flops 469827584 | bytes 7929856 | tf_op jit(solution)/shard_map/dot_general | solution.py:25
  35.9 0.0 reduce-scatter.4.cloned.1.call-update
  35.9 0.0 all-gather.6.cloned.1.call-start
  36.0 0.5 all-gather.6.cloned.1.call-update
  36.5 0.0 reduce-scatter.6.cloned.1.call-start
  36.5 0.0 copy-done.1
  36.6 0.2 fusion.9
  36.8 85.1 %all-reduce.1 = bf16[128,512]{1,0:T(8,128)(2,1)S(1)} all-reduce(f32[128,512]{1,0:T(8,128)S(1)} %fusion.9), channel_id=1, replica_groups=mesh['tp'=4,'row'=4,'col'=2] {'tp','row'}, use_global_device_ids=true, to_apply=%region_1.0 | all-reduce | flops 65536 | bytes 393216 | tf_op jit(solution)/shard_map/psum | solution.py:32
  121.9 0.0 reduce-scatter.4.cloned.1.call-done
  121.9 2.1 all_gather.13
  124.0 4.9 %convolution_convert_fusion.1 = bf16[256,4096]{1,0:T(8,128)(2,1)} fusion(bf16[4096,512]{1,0:T(8,128)(2,1)} %all-gather.6.cloned.1.call-done, bf16[128,256]{1,0:T(8,128)(2,1)S(1)} %all_gather.13, f32[256,512]{1,0:T(8,128)S(1)} %copy-done.3, bf16[128,512]{1,0:T(8,128)(2,1)S(1)} %all-reduce.1), kind=kOutput, calls=%fused_computation.1 | convolution fusion | flops 1108869120 | bytes 7012352 | tf_op jit(solution)/shard_map/dot_general | solution.py:16
  128.9 3.3 convert_element_type.30
  132.2 4.1 %copy.6 = bf16[256,4,2,512]{0,3,1,2:T(8,128)(2,1)} copy(bf16[256,4,2,512]{3,2,1,0:T(2,128)(2,1)S(1)} %convert_element_type.30) | data formatting | bytes 4194304 | tf_op jit(solution)/shard_map/convert_element_type | solution.py:40
  136.3 0.0 reduce-scatter.6.cloned.1.call-update
  136.4 0.0 all-gather.8.cloned.1.call-start
  136.4 6.9 %reduce-scatter.6.cloned.1.call-done = bf16[256,4,1,512]{0,3,1,2:T(8,128)(2,1)} async-done(((bf16[256,4,2,512]{0,3,1,2:T(8,128)(2,1)}), bf16[256,4,1,512]{0,3,1,2:T(8,128)(2,1)}) %reduce-scatter.6.cloned.1.call-update) | async-done | bytes 1048592 | tf_op jit(solution)/shard_map/reduce_scatter | solution.py:39
  143.3 0.0 all-gather.8.cloned.1.call-update
  143.4 0.0 reduce-scatter.8.cloned.1.call-start
  143.4 83.2 %all-gather.8.cloned.1.call-done = bf16[1024,2048]{0,1:T(8,128)(2,1)} async-done(((bf16[256,2048]{0,1:T(8,128)(2,1)}), bf16[1024,2048]{0,1:T(8,128)(2,1)}) %all-gather.8.cloned.1.call-update) | async-done | bytes 4194320 | tf_op jit(solution)/shard_map/all_gather | solution.py:43
  226.6 22.0 %convolution_convert_fusion = bf16[2048,3584]{1,0:T(8,128)(2,1)} fusion(bf16[1024,2048]{0,1:T(8,128)(2,1)} %all-gather.8.cloned.1.call-done, bf16[3584,1024]{1,0:T(8,128)(2,1)} %all-gather.4.cloned.1.call-done), kind=kOutput, calls=%fused_computation | convolution fusion | flops 15039725568 | bytes 26214400 | tf_op jit(solution)/shard_map/dot_general | solution.py:45
  248.6 0.0 reduce-scatter.8.cloned.1.call-update
  248.7 135.9 %reduce-scatter.8.cloned.1.call-done = bf16[512,3584]{1,0:T(8,128)(2,1)} async-done(((bf16[2048,3584]{1,0:T(8,128)(2,1)}), bf16[512,3584]{1,0:T(8,128)(2,1)}) %reduce-scatter.8.cloned.1.call-update) | async-done | bytes 3670032 | tf_op jit(solution)/shard_map/reduce_scatter | solution.py:44
  384.6 6.0 %convert_element_type.33 = f32[512,3584]{1,0:T(8,128)} convert(bf16[512,3584]{1,0:T(8,128)(2,1)} %reduce-scatter.8.cloned.1.call-done) | non-fusion elementwise | flops 1835008 | bytes 11010048 | tf_op jit(solution)/shard_map/convert_element_type | solution.py:51
  (3 shorter events, 0.0 us)
Async XLA Ops:
  7.4 23.4 %copy-start = (bf16[64,3584]{1,0:T(8,128)(2,1)S(1)}, bf16[64,3584]{1,0:T(8,128)(2,1)}, u32[]{:S(2)}) copy-start(bf16[64,3584]{1,0:T(8,128)(2,1)} %param.5) | copy-start | bytes 1376260
  7.4 23.4 %all-gather.4.cloned.1.call-start = ((), (), s32[]{:S(2)}) async-start(), calls=%async_computation.3 | async-start | bytes 11010048 | tf_op jit(solution)/shard_map/all_gather | solution.py:24
  8.1 28.5 %copy-start.1 = (bf16[256,512]{1,0:T(8,128)(2,1)S(1)}, bf16[256,512]{1,0:T(8,128)(2,1)}, u32[]{:S(2)}) copy-start(bf16[256,512]{1,0:T(8,128)(2,1)} %param.8) | copy-start | bytes 786436
  8.1 28.5 %copy-start.2 = (bf16[128,256]{1,0:T(8,128)(2,1)S(1)}, bf16[128,256]{1,0:T(8,128)(2,1)}, u32[]{:S(2)}) copy-start(bf16[128,256]{1,0:T(8,128)(2,1)} %param.6) | copy-start | bytes 196612
  8.1 115.9 %copy-start.3 = (f32[256,512]{1,0:T(8,128)S(1)}, f32[256,512]{1,0:T(8,128)}, u32[]{:S(2)}) copy-start(f32[256,512]{1,0:T(8,128)} %param.9) | copy-start | bytes 1572868
  8.1 113.8 %reduce-scatter.4.cloned.1.call-start = ((), (), s32[]{:S(2)}) async-start(), calls=%async_computation.4 | async-start | bytes 163840 | tf_op jit(solution)/shard_map/reduce_scatter | solution.py:26
  35.9 88.1 %all-gather.6.cloned.1.call-start = ((), (), s32[]{:S(2)}) async-start(), calls=%async_computation.5 | async-start | bytes 4456448 | tf_op jit(solution)/shard_map/all_gather | solution.py:35
  36.5 106.8 %reduce-scatter.6.cloned.1.call-start = ((), (), s32[]{:S(2)}) async-start(), calls=%async_computation.6 | async-start | bytes 3145728 | tf_op jit(solution)/shard_map/reduce_scatter | solution.py:39
  136.4 90.2 %all-gather.8.cloned.1.call-start = ((), (), s32[]{:S(2)}) async-start(), calls=%async_computation.7 | async-start | bytes 5242880 | tf_op jit(solution)/shard_map/all_gather | solution.py:43
  143.4 241.2 %reduce-scatter.8.cloned.1.call-start = ((), (), s32[]{:S(2)}) async-start(), calls=%async_computation.8 | async-start | bytes 18350080 | tf_op jit(solution)/shard_map/reduce_scatter | solution.py:44
Sparse Core Ops, SparseCore 0:
  9.7 21.0 all-gather.3
  36.0 21.2 reduce-scatter.3
  136.5 6.8 reduce-scatter.5
  144.7 81.7 all-gather.7
Sparse Core Ops, SparseCore 1:
  39.2 78.1 all-gather.5
  248.7 135.8 reduce-scatter.7
where the time goes:
time: 398 us
  waiting for transfers between devices  250 us (63%)
  blocking collectives  87.2 us (22%)
  matrix products  32.3 us (8%)
  between operations  14.7 us (4%)
  local copies, waits for them, and re-layouts  7.4 us (2%)
  other arithmetic  6.04 us (2%)
    reduce_scatter x1, waiting for transfers between devices, shards(): lax.psum_scatter(lax.dot_general(mixed, basis_block, (((0,), (1,)), ((),...  136 us
    psum x1, blocking collectives, shards(): rotated_out = lax.psum(partial_out, ('tp', 'row')).astype(jnp.bfloat16)  85.1 us
    all_gather x1, waiting for transfers between devices, shards(): mixed = lax.all_gather(mixed, 'row', axis=0, tiled=True)  83.2 us
    all_gather x1, waiting for transfers between devices, shards(): basis_block = lax.all_gather(basis_in, 'col', axis=0, tiled=True)  22.6 us
    dot_general x1, matrix products, shards(): lax.dot_general(mixed, basis_block, (((0,), (1,)), ((), ())), preferred_e...  22 us
  transfers between devices with their start and end apart: 6, of which 4 were waited for; matrix products, arithmetic and copies ran while one was open for 0% of the time, Pallas kernels for 0%

commit v1 on v0

--- a/solution.py
+++ b/solution.py
@@ -40,7 +40,9 @@
         mixed_part.astype(jnp.bfloat16), "col", scatter_dimension=2, tiled=True
     ).astype(jnp.float32)
     mixed = mixed.reshape(depth, width // col_count).astype(jnp.bfloat16)
-    mixed = lax.all_gather(mixed, "row", axis=0, tiled=True)
+    mixed = jnp.concatenate(
+        lax.all_to_all(jnp.stack([mixed] * lax.axis_size("row")), "row", 0, 0), axis=0
+    )
     return lax.psum_scatter(
         lax.dot_general(
             mixed, basis_block, (((0,), (1,)), ((), ())), preferred_element_type=jnp.float32

time: 398 us -> 415 us (1.043)
  blocking collectives: 87.2 us -> 185 us
  waiting for transfers between devices: 250 us -> 168 us
    all_to_all x0 -> x1, blocking collectives: none -> 98.2 us  [shards(): lax.all_to_all(jnp.stack([mixed] * lax.axis_size('row')), 'row', 0, 0)]
    all_gather x1 -> x0, waiting for transfers between devices: 83.2 us -> none  [shards(): mixed = lax.all_gather(mixed, 'row', axis=0, tiled=True)]
  transfers between devices with their start and end apart: 6 -> 5, of which waited for: 4 -> 3; matrix products, arithmetic and copies ran while one was open for 0% -> 0% of each run, Pallas kernels for 0% -> 0%
where the time goes in v1:
time: 415 us
  blocking collectives  185 us (45%)
  waiting for transfers between devices  168 us (40%)
  matrix products  31.4 us (8%)
  between operations  14.7 us (4%)
  local copies, waits for them, and re-layouts  9.4 us (2%)
  other arithmetic  6.04 us (1%)
    reduce_scatter x1, waiting for transfers between devices, shards(): lax.psum_scatter(lax.dot_general(mixed, basis_block, (((0,), (1,)), ((),...  137 us
    all_to_all x1, blocking collectives, shards(): lax.all_to_all(jnp.stack([mixed] * lax.axis_size('row')), 'row', 0, 0)  98.2 us
    psum x1, blocking collectives, shards(): rotated_out = lax.psum(partial_out, ('tp', 'row')).astype(jnp.bfloat16)  85.1 us
    all_gather x1, waiting for transfers between devices, shards(): basis_block = lax.all_gather(basis_in, 'col', axis=0, tiled=True)  22.6 us
    dot_general x1, matrix products, shards(): lax.dot_general(mixed, basis_block, (((0,), (1,)), ((), ())), preferred_e...  21.2 us
  transfers between devices with their start and end apart: 5, of which 3 were waited for; matrix products, arithmetic and copies ran while one was open for 0% of the time, Pallas kernels for 0%

profile of v1, /device:TPU:0, one launch (start us, length us, event | category | flops | bytes accessed | tf_op | source)
XLA Modules:
  0.0 414.7 jit_solution(7085943840375429739)
XLA Ops:
  7.4 0.0 copy-start
  7.4 0.0 all-gather.3.cloned.1.call-start
  7.4 0.7 all-gather.3.cloned.1.call-update
  8.1 0.0 copy-start.1
  8.1 0.0 copy-start.2
  8.1 0.0 copy-start.3
  8.1 0.0 reduce-scatter.4.cloned.1.call-start
  8.2 22.6 %all-gather.3.cloned.1.call-done = bf16[3584,1024]{1,0:T(8,128)(2,1)} async-done(((bf16[1792,1024]{1,0:T(8,128)(2,1)}), bf16[3584,1024]{1,0:T(8,128)(2,1)}) %all-gather.3.cloned.1.call-update) | async-done | bytes 7340048 | tf_op jit(solution)/shard_map/all_gather | solution.py:24
  30.8 0.0 copy-done
  30.8 5.1 %convolution_convert_fusion.2 = bf16[64,1024]{1,0:T(8,128)(2,1)} fusion(bf16[64,3584]{1,0:T(8,128)(2,1)S(1)} %copy-done, bf16[3584,1024]{1,0:T(8,128)(2,1)} %all-gather.3.cloned.1.call-done), kind=kOutput, calls=%fused_computation.4 | convolution fusion | flops 469827584 | bytes 7929856 | tf_op jit(solution)/shard_map/dot_general | solution.py:25
  35.9 0.0 reduce-scatter.4.cloned.1.call-update
  35.9 0.0 all-gather.5.cloned.1.call-start
  36.0 0.5 all-gather.5.cloned.1.call-update
  36.5 0.0 reduce-scatter.6.cloned.1.call-start
  36.5 0.0 copy-done.1
  36.6 0.2 fusion.9
  36.8 85.1 %all-reduce.1 = bf16[128,512]{1,0:T(8,128)(2,1)S(1)} all-reduce(f32[128,512]{1,0:T(8,128)S(1)} %fusion.9), channel_id=1, replica_groups=mesh['tp'=4,'row'=4,'col'=2] {'tp','row'}, use_global_device_ids=true, to_apply=%region_1.0 | all-reduce | flops 65536 | bytes 393216 | tf_op jit(solution)/shard_map/psum | solution.py:32
  121.9 0.0 reduce-scatter.4.cloned.1.call-done
  121.9 2.1 all_gather.10
  124.0 4.9 %convolution_convert_fusion.1 = bf16[256,4096]{1,0:T(8,128)(2,1)} fusion(bf16[4096,512]{1,0:T(8,128)(2,1)} %all-gather.5.cloned.1.call-done, bf16[128,256]{1,0:T(8,128)(2,1)S(1)} %all_gather.10, f32[256,512]{1,0:T(8,128)S(1)} %copy-done.3, bf16[128,512]{1,0:T(8,128)(2,1)S(1)} %all-reduce.1), kind=kOutput, calls=%fused_computation.1 | convolution fusion | flops 1108869120 | bytes 7012352 | tf_op jit(solution)/shard_map/dot_general | solution.py:16
  128.9 3.3 convert_element_type.32
  132.2 4.1 copy.6
  136.3 0.0 reduce-scatter.6.cloned.1.call-update
  136.4 0.0 reduce-scatter.8.cloned.1.call-start
  136.4 6.9 %reduce-scatter.6.cloned.1.call-done = bf16[256,4,1,512]{0,3,1,2:T(8,128)(2,1)} async-done(((bf16[256,4,2,512]{0,3,1,2:T(8,128)(2,1)}), bf16[256,4,1,512]{0,3,1,2:T(8,128)(2,1)}) %reduce-scatter.6.cloned.1.call-update) | async-done | bytes 1048592 | tf_op jit(solution)/shard_map/reduce_scatter | solution.py:39
  143.3 1.5 copy.7
  144.8 0.5 stack.2
  145.3 98.2 %all_to_all.5 = bf16[4,256,2048]{2,1,0:T(8,128)(2,1)S(1)} all-to-all(bf16[4,256,2048]{2,1,0:T(8,128)(2,1)S(1)} %stack.2), channel_id=1, replica_groups=mesh['tp'=4,'row'=4,'col'=2] {'row'}, dimensions={0} | all-to-all | bytes 8388608 | tf_op jit(solution)/shard_map/all_to_all | solution.py:44
  243.6 21.2 %convolution_convert_fusion = bf16[2048,3584]{1,0:T(8,128)(2,1)} fusion(bf16[1024,2048]{1,0:T(8,128)(2,1)S(1)} %bitcast.11, bf16[3584,1024]{1,0:T(8,128)(2,1)} %all-gather.3.cloned.1.call-done), kind=kOutput, calls=%fused_computation | convolution fusion | flops 15039725568 | bytes 26214400 | tf_op jit(solution)/shard_map/dot_general | solution.py:47
  264.7 0.0 reduce-scatter.8.cloned.1.call-update
  264.8 136.8 %reduce-scatter.8.cloned.1.call-done = bf16[512,3584]{1,0:T(8,128)(2,1)} async-done(((bf16[2048,3584]{1,0:T(8,128)(2,1)}), bf16[512,3584]{1,0:T(8,128)(2,1)}) %reduce-scatter.8.cloned.1.call-update) | async-done | bytes 3670032 | tf_op jit(solution)/shard_map/reduce_scatter | solution.py:46
  401.6 6.0 %convert_element_type.35 = f32[512,3584]{1,0:T(8,128)} convert(bf16[512,3584]{1,0:T(8,128)(2,1)} %reduce-scatter.8.cloned.1.call-done) | non-fusion elementwise | flops 1835008 | bytes 11010048 | tf_op jit(solution)/shard_map/convert_element_type | solution.py:53
  (3 shorter events, 0.0 us)
Async XLA Ops:
  7.4 23.4 %copy-start = (bf16[64,3584]{1,0:T(8,128)(2,1)S(1)}, bf16[64,3584]{1,0:T(8,128)(2,1)}, u32[]{:S(2)}) copy-start(bf16[64,3584]{1,0:T(8,128)(2,1)} %param.5) | copy-start | bytes 1376260
  7.4 23.4 %all-gather.3.cloned.1.call-start = ((), (), s32[]{:S(2)}) async-start(), calls=%async_computation.4 | async-start | bytes 11010048 | tf_op jit(solution)/shard_map/all_gather | solution.py:24
  8.1 28.5 %copy-start.1 = (bf16[256,512]{1,0:T(8,128)(2,1)S(1)}, bf16[256,512]{1,0:T(8,128)(2,1)}, u32[]{:S(2)}) copy-start(bf16[256,512]{1,0:T(8,128)(2,1)} %param.8) | copy-start | bytes 786436
  8.1 28.5 %copy-start.2 = (bf16[128,256]{1,0:T(8,128)(2,1)S(1)}, bf16[128,256]{1,0:T(8,128)(2,1)}, u32[]{:S(2)}) copy-start(bf16[128,256]{1,0:T(8,128)(2,1)} %param.6) | copy-start | bytes 196612
  8.1 115.9 %copy-start.3 = (f32[256,512]{1,0:T(8,128)S(1)}, f32[256,512]{1,0:T(8,128)}, u32[]{:S(2)}) copy-start(f32[256,512]{1,0:T(8,128)} %param.9) | copy-start | bytes 1572868
  8.1 113.8 %reduce-scatter.4.cloned.1.call-start = ((), (), s32[]{:S(2)}) async-start(), calls=%async_computation.5 | async-start | bytes 163840 | tf_op jit(solution)/shard_map/reduce_scatter | solution.py:26
  35.9 88.1 %all-gather.5.cloned.1.call-start = ((), (), s32[]{:S(2)}) async-start(), calls=%async_computation.6 | async-start | bytes 4456448 | tf_op jit(solution)/shard_map/all_gather | solution.py:35
  36.5 106.8 %reduce-scatter.6.cloned.1.call-start = ((), (), s32[]{:S(2)}) async-start(), calls=%async_computation.7 | async-start | bytes 3145728 | tf_op jit(solution)/shard_map/reduce_scatter | solution.py:39
  136.4 265.2 %reduce-scatter.8.cloned.1.call-start = ((), (), s32[]{:S(2)}) async-start(), calls=%async_computation.8 | async-start | bytes 18350080 | tf_op jit(solution)/shard_map/reduce_scatter | solution.py:46
Sparse Core Ops, SparseCore 0:
  9.7 21.0 all-gather.2
  36.0 21.2 reduce-scatter.3
  136.5 6.8 reduce-scatter.5
Sparse Core Ops, SparseCore 1:
  39.2 78.1 all-gather.4
  264.9 136.6 reduce-scatter.7
